TPU v7x, 256 devices: a whole 4x4x8 slice. The times are simulated.
256 devices in a mesh: dp: 32 (over x, z), expert: 8 (over y, core).
Axes of the slice: x: 4, y: 4, z: 8, core: 2. Of those that a mesh axis runs over, the one named last changes fastest.
Arguments:
- tokens: bfloat16 [32768, 2048], P(('dp', 'expert')), may hold values from -24 to 24
- expert_ids: int32 [32768, 4], P(('dp', 'expert')), may hold values from 0 to 7, all different within a row; in each aligned block of 128 rows (0 to 127, 128 to 255, ...) at most 128 rows name the same one
- gates: bfloat16 [32768, 4], P(('dp', 'expert')), may hold values from 0.099609375 to 1
- w_gate: bfloat16 [8, 2048, 384], P('expert'), may hold values from -0.125 to 0.125
- w_up: bfloat16 [8, 2048, 384], P('expert'), may hold values from -0.125 to 0.125
- w_down: bfloat16 [8, 384, 2048], P('expert'), may hold values from -0.3125 to 0.3125
- cotangent: bfloat16 [32768, 2048], P(('dp', 'expert')), may hold values from -6 to 6
Outputs:
- mixed: bfloat16 [32768, 2048], P(('dp', 'expert'))
- grad_tokens: bfloat16 [32768, 2048], P(('dp', 'expert'))
- grad_gate: float32 [8, 2048, 384], P('expert', 'dp')
- grad_up: float32 [8, 2048, 384], P('expert', 'dp')
- grad_down: float32 [8, 384, 2048], P('expert', 'dp')
Inputs may be any that keep to these rules, and one draw needn't show every extreme that they name: `expert_ids`: each row names 4 different experts. In each aligned block of 128 rows (the rows of one device) no expert is named by more than 128 rows, a bound that some block reaches.
All inputs are finite; a program needn't handle non-finite values.
Results may differ from a plain program's by a relative error of at most 0.024.
Values may be sent and summed in bfloat16 or wider, within the bound.
A program may use at most 128 MiB of HBM per device.

v0:
```python
import jax
import jax.numpy as jnp
from jax import lax
from jax.sharding import PartitionSpec as P


def expert_rows(inputs, out_grads, gate_col, gate_panel, up_panel, down_panel):
    pre_gate = jnp.dot(inputs, gate_panel, preferred_element_type=jnp.float32)
    pre_up = jnp.dot(inputs, up_panel, preferred_element_type=jnp.float32)
    gate_sigmoid = jax.nn.sigmoid(pre_gate)
    activated = (pre_gate * gate_sigmoid * pre_up).astype(jnp.bfloat16)
    expert_out = jnp.dot(activated, down_panel, preferred_element_type=jnp.float32)
    contrib = (gate_col.astype(jnp.float32)[:, None] * expert_out).astype(jnp.bfloat16)
    act_grad = lax.dot_general(
        out_grads, down_panel, (((1,), (1,)), ((), ())), preferred_element_type=jnp.float32
    )
    up_grad = (act_grad * pre_gate * gate_sigmoid).astype(jnp.bfloat16)
    pre_grad = (act_grad * pre_up * gate_sigmoid * (1.0 + pre_gate * (1.0 - gate_sigmoid))).astype(
        jnp.bfloat16
    )
    grad_rows = lax.dot_general(
        pre_grad, gate_panel, (((1,), (1,)), ((), ())), preferred_element_type=jnp.float32
    )
    grad_rows = grad_rows + lax.dot_general(
        up_grad, up_panel, (((1,), (1,)), ((), ())), preferred_element_type=jnp.float32
    )
    grad_rows = grad_rows.astype(jnp.bfloat16)
    wgrad_gate = lax.dot_general(
        inputs, pre_grad, (((0,), (0,)), ((), ())), preferred_element_type=jnp.float32
    )
    wgrad_up = lax.dot_general(
        inputs, up_grad, (((0,), (0,)), ((), ())), preferred_element_type=jnp.float32
    )
    wgrad_down = lax.dot_general(
        activated, out_grads, (((0,), (0,)), ((), ())), preferred_element_type=jnp.float32
    )
    return (contrib, grad_rows, wgrad_gate, wgrad_up, wgrad_down)


def slot_table(route_ids, expert_num, per_source):
    token_count, pick_count = route_ids.shape
    matches = route_ids == expert_num
    hit_rows = jnp.any(matches, axis=1).astype(jnp.int32)
    which_pick = jnp.sum(
        matches.astype(jnp.int32) * jnp.arange(pick_count, dtype=jnp.int32)[None, :], axis=1
    )
    rank_of = jnp.cumsum(hit_rows) - hit_rows
    wanted = jnp.arange(per_source, dtype=jnp.int32)
    chosen = ((hit_rows[None, :] == 1) & (rank_of[None, :] == wanted[:, None])).astype(jnp.int32)
    valid_slot = jnp.sum(chosen, axis=1) > 0
    row_of = jnp.sum(chosen * jnp.arange(token_count, dtype=jnp.int32)[None, :], axis=1)
    pick_of = jnp.sum(chosen * which_pick[None, :], axis=1)
    return (row_of, pick_of, valid_slot)


def per_device(tokens, expert_ids, gates, w_gate, w_up, w_down, cotangent):
    tok_dev, model_width = tokens.shape
    group_size = lax.axis_size("expert")
    slot_count = group_size * tok_dev
    my_expert = lax.axis_index("expert")
    gate_panel = w_gate[0]
    up_panel = w_up[0]
    down_panel = w_down[0]
    all_rows, all_cot, all_gates = (
        lax.all_gather(tokens, "expert", axis=0, tiled=True),
        lax.all_gather(cotangent, "expert", axis=0, tiled=True),
        lax.all_gather(gates, "expert", axis=0, tiled=True),
    )
    all_ids = lax.all_gather(expert_ids, "expert", axis=0, tiled=True)
    source_ids = all_ids.reshape(group_size, tok_dev, all_ids.shape[1])
    row_of, pick_of, keep_mask = jax.vmap(
        lambda route_ids: slot_table(route_ids, my_expert, tok_dev)
    )(source_ids)
    flat_row = (row_of + jnp.arange(group_size, dtype=jnp.int32)[:, None] * tok_dev).reshape(
        slot_count
    )
    keep_b = keep_mask.reshape(slot_count).astype(jnp.bfloat16)
    inputs = all_rows[flat_row] * keep_b[:, None]
    gate_col = all_gates[flat_row, pick_of.reshape(slot_count)] * keep_b
    out_grads = (
        gate_col.astype(jnp.float32)[:, None] * all_cot[flat_row].astype(jnp.float32)
    ).astype(jnp.bfloat16)
    contrib, grad_rows, acc_gate, acc_up, acc_down = expert_rows(
        inputs, out_grads, gate_col, gate_panel, up_panel, down_panel
    )
    dest = jnp.where(keep_mask.reshape(slot_count), flat_row, group_size * tok_dev)
    part_out = (
        jnp.zeros((group_size * tok_dev, model_width), jnp.float32)
        .at[dest]
        .set(contrib.astype(jnp.float32), mode="drop")
    )
    part_grad = (
        jnp.zeros((group_size * tok_dev, model_width), jnp.float32)
        .at[dest]
        .set(grad_rows.astype(jnp.float32), mode="drop")
    )
    summed_out, summed_grad = (
        lax.psum_scatter(
            part_out.astype(jnp.bfloat16), "expert", scatter_dimension=0, tiled=True
        ).astype(jnp.float32),
        lax.psum_scatter(
            part_grad.astype(jnp.bfloat16), "expert", scatter_dimension=0, tiled=True
        ).astype(jnp.float32),
    )
    mixed = summed_out.astype(jnp.bfloat16)
    grad_tokens = summed_grad.astype(jnp.bfloat16)
    grad_gate, grad_up, grad_down = (
        lax.psum_scatter(
            acc_gate.astype(jnp.bfloat16), "dp", scatter_dimension=0, tiled=True
        ).astype(jnp.float32),
        lax.psum_scatter(acc_up.astype(jnp.bfloat16), "dp", scatter_dimension=0, tiled=True).astype(
            jnp.float32
        ),
        lax.psum_scatter(
            acc_down.astype(jnp.bfloat16), "dp", scatter_dimension=0, tiled=True
        ).astype(jnp.float32),
    )
    return (mixed, grad_tokens, grad_gate[None], grad_up[None], grad_down[None])


def solution(mesh):
    return jax.shard_map(
        per_device,
        mesh=mesh,
        in_specs=(
            P(("dp", "expert"), None),
            P(("dp", "expert"), None),
            P(("dp", "expert"), None),
            P("expert", None, None),
            P("expert", None, None),
            P("expert", None, None),
            P(("dp", "expert"), None),
        ),
        out_specs=(
            P(("dp", "expert"), None),
            P(("dp", "expert"), None),
            P("expert", "dp", None),
            P("expert", "dp", None),
            P("expert", "dp", None),
        ),
        check_vma=False,
    )
```

profile of v0, /device:TPU:2, one launch (start us, length us, event | category | flops | bytes accessed | tf_op | source)
XLA Modules:
  0.0 633.2 jit_solution(9545320917792145153)
XLA Ops:
  8.7 12.2 %all_gather.12 = s32[1024,4]{0,1:T(4,128)S(1)} all-gather(s32[128,4]{0,1:T(4,128)} %param.8), channel_id=1, replica_groups=mesh['dp'=32,'expert'=8] {'expert'}, dimensions={0}, use_global_device_ids=true | all-gather | bytes 18432 | tf_op jit(solution)/shard_map/all_gather | solution.py:69
  21.3 9.9 %all_gather.13 = bf16[1024,4]{0,1:T(4,128)(2,1)S(1)} all-gather(bf16[128,4]{0,1:T(4,128)(2,1)} %param.9), channel_id=1, replica_groups=mesh['dp'=32,'expert'=8] {'expert'}, dimensions={0}, use_global_device_ids=true | all-gather | bytes 9216 | tf_op jit(solution)/shard_map/all_gather | solution.py:67
  31.8 9.1 %gather_fusion = bf16[1024]{0:T(1024)(128)(2,1)S(1)} fusion(bf16[1024,4]{0,1:T(4,128)(2,1)S(1)} %all_gather.13, s32[1024]{0:T(1024)S(1)} %bitcast.63), kind=kCustom, calls=%fused_computation | custom fusion | bytes 12288 | tf_op jit(solution)/shard_map/gather | solution.py:79
  40.9 6.6 %all-gather.3.cloned.1.call-done = bf16[1024,2048]{1,0:T(8,128)(2,1)} async-done(((bf16[128,2048]{1,0:T(8,128)(2,1)}), bf16[1024,2048]{1,0:T(8,128)(2,1)}) %all-gather.3.cloned.1.call-update) | async-done | bytes 4194320 | tf_op jit(solution)/shard_map/all_gather | solution.py:65
  47.6 11.5 %gather_fusion.1 = bf16[1024,2048]{1,0:T(8,128)(2,1)} fusion(bf16[1024,2048]{1,0:T(8,128)(2,1)} %all-gather.3.cloned.1.call-done, s32[1024]{0:T(1024)S(1)} %broadcast_clamp_fusion), kind=kCustom, calls=%fused_computation.1 | custom fusion | bytes 8392704 | tf_op jit(solution)/shard_map/gather | solution.py:78
  59.1 6.6 %fusion.9 = f32[1024,384]{1,0:T(8,128)} fusion(bf16[1024,2048]{1,0:T(8,128)(2,1)} %gather_fusion.1, bf16[1024]{0:T(1024)(128)(2,1)S(1)} %bitcast_convert_fusion.2, bf16[1,2048,384]{2,1,0:T(8,128)(2,1)} %param.11), kind=kOutput, calls=%fused_computation.19 | convolution fusion | flops 1612709888 | bytes 7342080 | tf_op jit(solution)/shard_map/dot_general | solution.py:9
  69.3 14.8 %all-gather.5.cloned.1.call-done = bf16[1024,2048]{1,0:T(8,128)(2,1)} async-done(((bf16[128,2048]{1,0:T(8,128)(2,1)}), bf16[1024,2048]{1,0:T(8,128)(2,1)}) %all-gather.5.cloned.1.call-update) | async-done | bytes 4194320 | tf_op jit(solution)/shard_map/all_gather | solution.py:66
  84.1 11.5 %gather_fusion.2 = bf16[1024,2048]{1,0:T(8,128)(2,1)} fusion(bf16[1024,2048]{1,0:T(8,128)(2,1)} %all-gather.5.cloned.1.call-done, s32[1024]{0:T(1024)S(1)} %broadcast_clamp_fusion), kind=kCustom, calls=%fused_computation.2 | custom fusion | bytes 8392704 | tf_op jit(solution)/shard_map/gather | solution.py:81
  95.6 7.3 %multiply_convert_fusion.4 = (bf16[1024,384]{1,0:T(8,128)(2,1)S(1)}, bf16[1024,384]{1,0:T(8,128)(2,1)}, bf16[1024,384]{1,0:T(8,128)(2,1)}) fusion(f32[1024,384]{1,0:T(8,128)} %fusion.11, f32[1024,384]{1,0:T(8,128)} %fusion.9, bf16[1,384,2048]{2,1,0:T(8,128)(2,1)S(1)} %copy-done, bf16[1024,2048]{1,0:T(8,128)(2,1)} %gather_fusion.2, ...), kind=kOutput, calls=%fused_computation.35 | convolution fusion | flops 1623195648 | bytes 11276288 | tf_op jit(solution)/shard_map/dot_general | solution.py:14
  107.9 6.1 convolution_convert_fusion.2
  114.1 5.4 multiply_convert_fusion.1
  119.5 10.9 %scatter_custom_fusion = f32[1024,2048]{1,0:T(8,128)} fusion(s32[1024]{0:T(1024)S(1)} %bitcast.70, bf16[1024,2048]{1,0:T(8,128)(2,1)} %multiply_convert_fusion.1, f32[]{:T(128)} %constant.10.clone.1), kind=kCustom, calls=%fused_computation.9 | custom fusion | flops 2097152 | bytes 12582916 | tf_op jit(solution)/shard_map/scatter | solution.py:90
  130.4 6.0 convert_element_type.93
  140.4 4.3 add_convert_fusion
  144.7 11.0 %scatter_custom_fusion.1 = f32[1024,2048]{1,0:T(8,128)} fusion(s32[1024]{0:T(1024)S(1)} %bitcast.71, bf16[1024,2048]{1,0:T(8,128)(2,1)} %add_convert_fusion, f32[]{:T(128)} %constant.10.clone.1), kind=kCustom, calls=%fused_computation.5 | custom fusion | flops 2097152 | bytes 12582916 | tf_op jit(solution)/shard_map/scatter | solution.py:95
  155.7 6.0 convert_element_type.100
  161.7 4.4 convolution_convert_fusion
  166.2 78.7 %fusion = bf16[16,2048]{1,0:T(8,128)(2,1)S(1)} fusion(bf16[384,2048]{1,0:T(8,128)(2,1)S(1)} %convolution_convert_fusion), kind=kCustom, calls=%all-reduce-scatter | all-reduce-scatter fusion | flops 1048577 | bytes 1639424
  249.4 10.2 %collective-permute-start.7 = (bf16[12,2048]{1,0:T(8,128)(2,1)S(1)}, bf16[12,2048]{1,0:T(8,128)(2,1)S(1)}, u32[]{:S(2)}, u32[]{:S(2)}) collective-permute-start(bf16[12,2048]{1,0:T(8,128)(2,1)S(1)} %slice.6), channel_id=1, source_target_pairs={{0,64},{8,72},{16,80},{24,88},{32,96},{40,104},{48,112},{56,120},{... | collective-permute-start | bytes 147464
  261.4 9.1 %collective-permute-start.3 = (bf16[16,2048]{1,0:T(8,128)(2,1)S(1)}, bf16[16,2048]{1,0:T(8,128)(2,1)S(1)}, u32[]{:S(2)}, u32[]{:S(2)}) collective-permute-start(bf16[16,2048]{1,0:T(8,128)(2,1)S(1)} %fusion), channel_id=1, source_target_pairs={{0,32},{8,40},{16,48},{24,56},{32,64},{40,72},{48,80},{56,88},{64,... | collective-permute-start | bytes 196616
  287.0 36.3 %reduce-scatter.13.cloned.1.call-done = bf16[64,384]{1,0:T(8,128)(2,1)} async-done(((bf16[2048,384]{1,0:T(8,128)(2,1)}), bf16[64,384]{1,0:T(8,128)(2,1)}) %reduce-scatter.13.cloned.1.call-update) | async-done | bytes 49168 | tf_op jit(solution)/shard_map/reduce_scatter | solution.py:111
  324.7 216.6 %reduce-scatter.11.cloned.1.call-done = bf16[64,384]{1,0:T(8,128)(2,1)} async-done(((bf16[2048,384]{1,0:T(8,128)(2,1)}), bf16[64,384]{1,0:T(8,128)(2,1)}) %reduce-scatter.11.cloned.1.call-update) | async-done | bytes 49168 | tf_op jit(solution)/shard_map/reduce_scatter | solution.py:108
  542.8 41.2 %reduce-scatter.7.cloned.1.call-done = bf16[128,2048]{1,0:T(8,128)(2,1)} async-done(((bf16[1024,2048]{1,0:T(8,128)(2,1)}), bf16[128,2048]{1,0:T(8,128)(2,1)}) %reduce-scatter.7.cloned.1.call-update) | async-done | bytes 524304 | tf_op jit(solution)/shard_map/reduce_scatter | solution.py:98
  584.0 42.3 %reduce-scatter.9.cloned.1.call-done = bf16[128,2048]{1,0:T(8,128)(2,1)} async-done(((bf16[1024,2048]{1,0:T(8,128)(2,1)}), bf16[128,2048]{1,0:T(8,128)(2,1)}) %reduce-scatter.9.cloned.1.call-update) | async-done | bytes 524304 | tf_op jit(solution)/shard_map/reduce_scatter | solution.py:101
  (66 shorter events, 39.9 us)
Async XLA Ops:
  7.2 88.5 %copy-start = (bf16[1,384,2048]{2,1,0:T(8,128)(2,1)S(1)}, bf16[1,384,2048]{2,1,0:T(8,128)(2,1)}, u32[]{:S(2)}) copy-start(bf16[1,384,2048]{2,1,0:T(8,128)(2,1)} %param.12) | copy-start | bytes 4718596
  7.2 40.4 %all-gather.3.cloned.1.call-start = ((), (), s32[]{:S(2)}) async-start(), calls=%async_computation.4 | async-start | bytes 4718592 | tf_op jit(solution)/shard_map/all_gather | solution.py:65
  7.9 76.2 %all-gather.5.cloned.1.call-start = ((), (), s32[]{:S(2)}) async-start(), calls=%async_computation.6 | async-start | bytes 4718592 | tf_op jit(solution)/shard_map/all_gather | solution.py:66
  8.7 314.6 %reduce-scatter.13.cloned.1.call-start = ((), (), s32[]{:S(2)}) async-start(), calls=%async_computation.9 | async-start | bytes 1622016 | tf_op jit(solution)/shard_map/reduce_scatter | solution.py:111
  59.1 6.6 %copy-start.1 = (bf16[1024,2048]{1,0:T(8,128)(2,1)S(1)}, bf16[1024,2048]{1,0:T(8,128)(2,1)}, u32[]{:S(2)}) copy-start(bf16[1024,2048]{1,0:T(8,128)(2,1)} %gather_fusion.1) | copy-start | bytes 12582916
  59.1 6.6 %copy-start.3 = (bf16[1,2048,384]{2,1,0:T(8,128)(2,1)S(1)}, bf16[1,2048,384]{2,1,0:T(8,128)(2,1)}, u32[]{:S(2)}) copy-start(bf16[1,2048,384]{2,1,0:T(8,128)(2,1)} %param.10) | copy-start | bytes 4718596
  95.6 8.2 %copy-start.2 = (bf16[1024,2048]{1,0:T(8,128)(2,1)S(1)}, bf16[1024,2048]{1,0:T(8,128)(2,1)}, u32[]{:S(2)}) copy-start(bf16[1024,2048]{1,0:T(8,128)(2,1)} %gather_fusion.1) | copy-start | bytes 12582916
  103.0 0.9 copy-start.5
  107.7 433.7 %reduce-scatter.11.cloned.1.call-start = ((), (), s32[]{:S(2)}) async-start(), calls=%async_computation.8 | async-start | bytes 1622016 | tf_op jit(solution)/shard_map/reduce_scatter | solution.py:108
  114.0 470.0 %reduce-scatter.7.cloned.1.call-start = ((), (), s32[]{:S(2)}) async-start(), calls=%async_computation.5 | async-start | bytes 4718592 | tf_op jit(solution)/shard_map/reduce_scatter | solution.py:98
  136.4 489.9 %reduce-scatter.9.cloned.1.call-start = ((), (), s32[]{:S(2)}) async-start(), calls=%async_computation.7 | async-start | bytes 4718592 | tf_op jit(solution)/shard_map/reduce_scatter | solution.py:101
  136.7 3.7 copy-start.4
  136.7 3.7 copy-start.6
  161.7 118.2 %copy-start.7 = (u32[256]{0:T(256)S(1)}, u32[256]{0:T(256)}, u32[]{:S(2)}) copy-start(u32[256]{0:T(256)} %constant.53) | copy-start | bytes 3076
  244.9 27.6 %collective-permute-start.6 = (bf16[16,2048]{1,0:T(8,128)(2,1)S(1)}, bf16[16,2048]{1,0:T(8,128)(2,1)S(1)}, u32[]{:S(2)}, u32[]{:S(2)}) collective-permute-start(bf16[16,2048]{1,0:T(8,128)(2,1)S(1)} %fusion), channel_id=1, source_target_pairs={{0,56},{8,64},{16,72},{24,80},{32,88},{40,96},{48,104},{56,112},{6... | collective-permute-start | bytes 196616
  247.4 29.1 %collective-permute-start.5 = (bf16[16,2048]{1,0:T(8,128)(2,1)S(1)}, bf16[16,2048]{1,0:T(8,128)(2,1)S(1)}, u32[]{:S(2)}, u32[]{:S(2)}) collective-permute-start(bf16[16,2048]{1,0:T(8,128)(2,1)S(1)} %fusion), channel_id=1, source_target_pairs={{0,48},{8,56},{16,64},{24,72},{32,80},{40,88},{48,96},{56,104},{64... | collective-permute-start | bytes 196616
  249.4 21.2 %collective-permute-start.7 = (bf16[12,2048]{1,0:T(8,128)(2,1)S(1)}, bf16[12,2048]{1,0:T(8,128)(2,1)S(1)}, u32[]{:S(2)}, u32[]{:S(2)}) collective-permute-start(bf16[12,2048]{1,0:T(8,128)(2,1)S(1)} %slice.6), channel_id=1, source_target_pairs={{0,64},{8,72},{16,80},{24,88},{32,96},{40,104},{48,112},{56,120},{... | collective-permute-start | bytes 147464
  259.5 21.6 %collective-permute-start.4 = (bf16[16,2048]{1,0:T(8,128)(2,1)S(1)}, bf16[16,2048]{1,0:T(8,128)(2,1)S(1)}, u32[]{:S(2)}, u32[]{:S(2)}) collective-permute-start(bf16[16,2048]{1,0:T(8,128)(2,1)S(1)} %fusion), channel_id=1, source_target_pairs={{0,40},{8,48},{16,56},{24,64},{32,72},{40,80},{48,88},{56,96},{64,... | collective-permute-start | bytes 196616
  261.4 19.7 %collective-permute-start.3 = (bf16[16,2048]{1,0:T(8,128)(2,1)S(1)}, bf16[16,2048]{1,0:T(8,128)(2,1)S(1)}, u32[]{:S(2)}, u32[]{:S(2)}) collective-permute-start(bf16[16,2048]{1,0:T(8,128)(2,1)S(1)} %fusion), channel_id=1, source_target_pairs={{0,32},{8,40},{16,48},{24,56},{32,64},{40,72},{48,80},{56,88},{64,... | collective-permute-start | bytes 196616
  270.6 10.6 %collective-permute-start.2 = (bf16[16,2048]{1,0:T(8,128)(2,1)S(1)}, bf16[16,2048]{1,0:T(8,128)(2,1)S(1)}, u32[]{:S(2)}, u32[]{:S(2)}) collective-permute-start(bf16[16,2048]{1,0:T(8,128)(2,1)S(1)} %fusion), channel_id=1, source_target_pairs={{0,24},{8,32},{16,40},{24,48},{32,56},{40,64},{48,72},{56,80},{64,... | collective-permute-start | bytes 196616
  272.5 10.9 %collective-permute-start.1 = (bf16[16,2048]{1,0:T(8,128)(2,1)S(1)}, bf16[16,2048]{1,0:T(8,128)(2,1)S(1)}, u32[]{:S(2)}, u32[]{:S(2)}) collective-permute-start(bf16[16,2048]{1,0:T(8,128)(2,1)S(1)} %fusion), channel_id=1, source_target_pairs={{0,16},{8,24},{16,32},{24,40},{32,48},{40,56},{48,64},{56,72},{64,... | collective-permute-start | bytes 196616
  276.5 8.3 %collective-permute-start = (bf16[16,2048]{1,0:T(8,128)(2,1)S(1)}, bf16[16,2048]{1,0:T(8,128)(2,1)S(1)}, u32[]{:S(2)}, u32[]{:S(2)}) collective-permute-start(bf16[16,2048]{1,0:T(8,128)(2,1)S(1)} %fusion), channel_id=1, source_target_pairs={{0,8},{8,16},{16,24},{24,32},{32,40},{40,48},{48,56},{56,64},{64,7... | collective-permute-start | bytes 196616
Sparse Core Ops, SparseCore 0:
  9.9 37.6 all-gather.2
  49.4 34.6 all-gather.4
  107.8 215.4 reduce-scatter.12
  327.0 214.3 reduce-scatter.10
  544.4 39.5 reduce-scatter.6
  587.0 39.3 reduce-scatter.8
where the time goes:
time: 634 us; the launch traced here: 633 us
  waiting for transfers between devices  363 us (57%)
  blocking collectives  101 us (16%)
  matrix products  45.2 us (7%)
  other arithmetic  37.8 us (6%)
  local copies, waits for them, and re-layouts  35.9 us (6%)
  starting transfers between devices  35.5 us (6%)
  between operations  15.1 us (2%)
    reduce_scatter x1, waiting for transfers between devices, per_device(): lax.psum_scatter(acc_gate.astype(jnp.bfloat16), 'dp', scatter_dimension=0...  217 us
    unnamed x1, blocking collectives  78.7 us
    reduce_scatter x1, waiting for transfers between devices, per_device(): lax.psum_scatter(part_grad.astype(jnp.bfloat16), 'expert', scatter_dimens...  42.3 us
    reduce_scatter x1, waiting for transfers between devices, per_device(): lax.psum_scatter(part_out.astype(jnp.bfloat16), 'expert', scatter_dimensi...  41.2 us
    reduce_scatter x1, waiting for transfers between devices, per_device(): lax.psum_scatter(acc_up.astype(jnp.bfloat16), 'dp', scatter_dimension=0,...  36.3 us
    unnamed x8, starting transfers between devices  34.9 us
    all_gather x1, waiting for transfers between devices, per_device(): lax.all_gather(cotangent, 'expert', axis=0, tiled=True)  14.8 us
  transfers between devices with their start and end apart: 14, of which 8 were waited for; matrix products, arithmetic and copies ran while one was open for 27% of the time, Pallas kernels for 0%

commit v1 on v0

--- a/solution.py
+++ b/solution.py
@@ -63,7 +63,9 @@
     down_panel = w_down[0]
     all_rows, all_cot, all_gates = (
         lax.all_gather(tokens, "expert", axis=0, tiled=True),
-        lax.all_gather(cotangent, "expert", axis=0, tiled=True),
+        jnp.concatenate(
+            lax.all_to_all(jnp.stack([cotangent] * lax.axis_size("expert")), "expert", 0, 0), axis=0
+        ),
         lax.all_gather(gates, "expert", axis=0, tiled=True),
     )
     all_ids = lax.all_gather(expert_ids, "expert", axis=0, tiled=True)

time: 634 us -> 673 us (1.062)
  blocking collectives: 101 us -> 163 us
  waiting for transfers between devices: 363 us -> 339 us
    all_gather x1, blocking collectives: 12.2 us -> 71 us  [per_device(): all_ids = lax.all_gather(expert_ids, 'expert', axis=0, tiled=True)]
    all_gather x1 -> x0, waiting for transfers between devices: 14.8 us -> none  [per_device(): lax.all_gather(cotangent, 'expert', axis=0, tiled=True)]
  transfers between devices with their start and end apart: 14 -> 14, of which waited for: 8 -> 6; matrix products, arithmetic and copies ran while one was open for 27% -> 25% of each run, Pallas kernels for 0% -> 0%
where the time goes in v1:
time: 673 us; the launch traced here: 672 us
  waiting for transfers between devices  339 us (50%)
  blocking collectives  163 us (24%)
  local copies, waits for them, and re-layouts  39.4 us (6%)
  matrix products  39.3 us (6%)
  starting transfers between devices  39 us (6%)
  other arithmetic  37.8 us (6%)
  between operations  14.8 us (2%)
    reduce_scatter x1, waiting for transfers between devices, per_device(): lax.psum_scatter(acc_gate.astype(jnp.bfloat16), 'dp', scatter_dimension=0...  217 us
    unnamed x1, blocking collectives  82 us
    all_gather x1, blocking collectives, per_device(): all_ids = lax.all_gather(expert_ids, 'expert', axis=0, tiled=True)  71 us
    reduce_scatter x1, waiting for transfers between devices, per_device(): lax.psum_scatter(part_grad.astype(jnp.bfloat16), 'expert', scatter_dimens...  42.3 us
    reduce_scatter x1, waiting for transfers between devices, per_device(): lax.psum_scatter(part_out.astype(jnp.bfloat16), 'expert', scatter_dimensi...  41.1 us
    reduce_scatter x1, waiting for transfers between devices, per_device(): lax.psum_scatter(acc_up.astype(jnp.bfloat16), 'dp', scatter_dimension=0,...  34.8 us
    unnamed x8, starting transfers between devices  33.7 us
  transfers between devices with their start and end apart: 14, of which 6 were waited for; matrix products, arithmetic and copies ran while one was open for 25% of the time, Pallas kernels for 0%

profile of v1, /device:TPU:2, one launch (start us, length us, event | category | flops | bytes accessed | tf_op | source)
XLA Modules:
  0.0 672.5 jit_solution(13478985650277986934)
XLA Ops:
  11.4 4.7 all-to-all-start
  16.2 71.0 %all_gather.9 = s32[1024,4]{0,1:T(4,128)S(1)} all-gather(s32[128,4]{0,1:T(4,128)S(1)} %copy-done.7), channel_id=1, replica_groups=mesh['dp'=32,'expert'=8] {'expert'}, dimensions={0}, use_global_device_ids=true | all-gather | bytes 18432 | tf_op jit(solution)/shard_map/all_gather | solution.py:71
  87.5 9.9 %all_gather.10 = bf16[1024,4]{0,1:T(4,128)(2,1)S(1)} all-gather(bf16[128,4]{0,1:T(4,128)(2,1)S(1)} %copy-done.8), channel_id=1, replica_groups=mesh['dp'=32,'expert'=8] {'expert'}, dimensions={0}, use_global_device_ids=true | all-gather | bytes 9216 | tf_op jit(solution)/shard_map/all_gather | solution.py:69
  98.1 9.1 %gather_fusion = bf16[1024]{0:T(1024)(128)(2,1)S(1)} fusion(bf16[1024,4]{0,1:T(4,128)(2,1)S(1)} %all_gather.10, s32[1024]{0:T(1024)S(1)} %bitcast.64), kind=kCustom, calls=%fused_computation | custom fusion | bytes 12288 | tf_op jit(solution)/shard_map/gather | solution.py:81
  107.2 11.5 %gather_fusion.2 = bf16[1024,2048]{1,0:T(8,128)(2,1)} fusion(bf16[1024,2048]{1,0:T(8,128)(2,1)} %bitcast.11, s32[1024]{0:T(1024)S(1)} %broadcast_clamp_fusion), kind=kCustom, calls=%fused_computation.2 | custom fusion | bytes 8392704 | tf_op jit(solution)/shard_map/gather | solution.py:83
  118.7 11.5 %gather_fusion.1 = bf16[1024,2048]{1,0:T(8,128)(2,1)} fusion(bf16[1024,2048]{1,0:T(8,128)(2,1)} %all-gather.2.cloned.1.call-done, s32[1024]{0:T(1024)S(1)} %broadcast_clamp_fusion), kind=kCustom, calls=%fused_computation.1 | custom fusion | bytes 8392704 | tf_op jit(solution)/shard_map/gather | solution.py:80
  130.3 5.2 fusion.9
  137.9 4.1 multiply_convert_fusion.4
  146.9 6.1 convolution_convert_fusion.2
  153.1 5.4 multiply_convert_fusion.1
  158.5 10.9 %scatter_custom_fusion = f32[1024,2048]{1,0:T(8,128)} fusion(s32[1024]{0:T(1024)S(1)} %bitcast.71, bf16[1024,2048]{1,0:T(8,128)(2,1)} %multiply_convert_fusion.1, f32[]{:T(128)} %constant.10.clone.1), kind=kCustom, calls=%fused_computation.9 | custom fusion | flops 2097152 | bytes 12582916 | tf_op jit(solution)/shard_map/scatter | solution.py:92
  169.4 6.0 convert_element_type.93
  179.4 4.3 add_convert_fusion
  183.7 10.9 %scatter_custom_fusion.1 = f32[1024,2048]{1,0:T(8,128)} fusion(s32[1024]{0:T(1024)S(1)} %bitcast.72, bf16[1024,2048]{1,0:T(8,128)(2,1)} %add_convert_fusion, f32[]{:T(128)} %constant.10.clone.1), kind=kCustom, calls=%fused_computation.5 | custom fusion | flops 2097152 | bytes 12582916 | tf_op jit(solution)/shard_map/scatter | solution.py:97
  194.7 6.0 convert_element_type.100
  200.7 4.4 convolution_convert_fusion
  205.2 82.0 %fusion = bf16[16,2048]{1,0:T(8,128)(2,1)S(1)} fusion(bf16[384,2048]{1,0:T(8,128)(2,1)S(1)} %convolution_convert_fusion), kind=kCustom, calls=%all-reduce-scatter | all-reduce-scatter fusion | flops 1048577 | bytes 1639424
  291.1 9.5 %collective-permute-start.7 = (bf16[12,2048]{1,0:T(8,128)(2,1)S(1)}, bf16[12,2048]{1,0:T(8,128)(2,1)S(1)}, u32[]{:S(2)}, u32[]{:S(2)}) collective-permute-start(bf16[12,2048]{1,0:T(8,128)(2,1)S(1)} %slice.6), channel_id=1, source_target_pairs={{0,64},{8,72},{16,80},{24,88},{32,96},{40,104},{48,112},{56,120},{... | collective-permute-start | bytes 147464
  302.5 9.1 %collective-permute-start.3 = (bf16[16,2048]{1,0:T(8,128)(2,1)S(1)}, bf16[16,2048]{1,0:T(8,128)(2,1)S(1)}, u32[]{:S(2)}, u32[]{:S(2)}) collective-permute-start(bf16[16,2048]{1,0:T(8,128)(2,1)S(1)} %fusion), channel_id=1, source_target_pairs={{0,32},{8,40},{16,48},{24,56},{32,64},{40,72},{48,80},{56,88},{64,... | collective-permute-start | bytes 196616
  313.6 4.0 collective-permute-start.1
  328.1 34.8 %reduce-scatter.13.cloned.1.call-done = bf16[64,384]{1,0:T(8,128)(2,1)} async-done(((bf16[2048,384]{1,0:T(8,128)(2,1)}), bf16[64,384]{1,0:T(8,128)(2,1)}) %reduce-scatter.13.cloned.1.call-update) | async-done | bytes 49168 | tf_op jit(solution)/shard_map/reduce_scatter | solution.py:113
  364.4 216.8 %reduce-scatter.11.cloned.1.call-done = bf16[64,384]{1,0:T(8,128)(2,1)} async-done(((bf16[2048,384]{1,0:T(8,128)(2,1)}), bf16[64,384]{1,0:T(8,128)(2,1)}) %reduce-scatter.11.cloned.1.call-update) | async-done | bytes 49168 | tf_op jit(solution)/shard_map/reduce_scatter | solution.py:110
  582.6 41.1 %reduce-scatter.7.cloned.1.call-done = bf16[128,2048]{1,0:T(8,128)(2,1)} async-done(((bf16[1024,2048]{1,0:T(8,128)(2,1)}), bf16[128,2048]{1,0:T(8,128)(2,1)}) %reduce-scatter.7.cloned.1.call-update) | async-done | bytes 524304 | tf_op jit(solution)/shard_map/reduce_scatter | solution.py:100
  623.7 42.3 %reduce-scatter.9.cloned.1.call-done = bf16[128,2048]{1,0:T(8,128)(2,1)} async-done(((bf16[1024,2048]{1,0:T(8,128)(2,1)}), bf16[128,2048]{1,0:T(8,128)(2,1)}) %reduce-scatter.9.cloned.1.call-update) | async-done | bytes 524304 | tf_op jit(solution)/shard_map/reduce_scatter | solution.py:103
  (70 shorter events, 36.9 us)
Async XLA Ops:
  7.2 130.7 %copy-start = (bf16[1,384,2048]{2,1,0:T(8,128)(2,1)S(1)}, bf16[1,384,2048]{2,1,0:T(8,128)(2,1)}, u32[]{:S(2)}) copy-start(bf16[1,384,2048]{2,1,0:T(8,128)(2,1)} %param.12) | copy-start | bytes 4718596
  7.2 111.5 %all-gather.2.cloned.1.call-start = ((), (), s32[]{:S(2)}) async-start(), calls=%async_computation.5 | async-start | bytes 4718592 | tf_op jit(solution)/shard_map/all_gather | solution.py:65
  11.4 4.7 copy-start.7
  11.4 76.1 %copy-start.8 = (bf16[128,4]{0,1:T(4,128)(2,1)S(1)}, bf16[128,4]{0,1:T(4,128)(2,1)}, u32[]{:S(2)}) copy-start(bf16[128,4]{0,1:T(4,128)(2,1)} %param.9) | copy-start | bytes 3076
  11.4 95.7 %all-to-all-start = ((bf16[8,128,2048]{2,1,0:T(8,128)(2,1)}), bf16[8,128,2048]{2,1,0:T(8,128)(2,1)}, u32[]{:S(2)}, u32[]{:S(2)}) async-start(bf16[8,128,2048]{2,1,0:T(8,128)(2,1)} %stack.2), calls=%async_computation.1 | async-start | bytes 8388608 | tf_op jit(solution)/shard_map/all_to_all | solution.py:67
  16.1 346.8 %reduce-scatter.13.cloned.1.call-start = ((), (), s32[]{:S(2)}) async-start(), calls=%async_computation.9 | async-start | bytes 1622016 | tf_op jit(solution)/shard_map/reduce_scatter | solution.py:113
  130.2 5.2 copy-start.2
  130.2 5.2 copy-start.3
  135.5 2.4 copy-start.1
  142.0 0.9 copy-start.5
  146.7 434.5 %reduce-scatter.11.cloned.1.call-start = ((), (), s32[]{:S(2)}) async-start(), calls=%async_computation.8 | async-start | bytes 1622016 | tf_op jit(solution)/shard_map/reduce_scatter | solution.py:110
  153.0 470.7 %reduce-scatter.7.cloned.1.call-start = ((), (), s32[]{:S(2)}) async-start(), calls=%async_computation.6 | async-start | bytes 4718592 | tf_op jit(solution)/shard_map/reduce_scatter | solution.py:100
  175.4 490.5 %reduce-scatter.9.cloned.1.call-start = ((), (), s32[]{:S(2)}) async-start(), calls=%async_computation.7 | async-start | bytes 4718592 | tf_op jit(solution)/shard_map/reduce_scatter | solution.py:103
  175.7 3.7 copy-start.4
  175.7 3.7 copy-start.6
  200.7 120.3 %copy-start.9 = (u32[256]{0:T(256)S(1)}, u32[256]{0:T(256)}, u32[]{:S(2)}) copy-start(u32[256]{0:T(256)} %constant.53) | copy-start | bytes 3076
  287.2 26.4 %collective-permute-start.6 = (bf16[16,2048]{1,0:T(8,128)(2,1)S(1)}, bf16[16,2048]{1,0:T(8,128)(2,1)S(1)}, u32[]{:S(2)}, u32[]{:S(2)}) collective-permute-start(bf16[16,2048]{1,0:T(8,128)(2,1)S(1)} %fusion), channel_id=1, source_target_pairs={{0,56},{8,64},{16,72},{24,80},{32,88},{40,96},{48,104},{56,112},{6... | collective-permute-start | bytes 196616
  289.1 28.5 %collective-permute-start.5 = (bf16[16,2048]{1,0:T(8,128)(2,1)S(1)}, bf16[16,2048]{1,0:T(8,128)(2,1)S(1)}, u32[]{:S(2)}, u32[]{:S(2)}) collective-permute-start(bf16[16,2048]{1,0:T(8,128)(2,1)S(1)} %fusion), channel_id=1, source_target_pairs={{0,48},{8,56},{16,64},{24,72},{32,80},{40,88},{48,96},{56,104},{64... | collective-permute-start | bytes 196616
  291.1 20.6 %collective-permute-start.7 = (bf16[12,2048]{1,0:T(8,128)(2,1)S(1)}, bf16[12,2048]{1,0:T(8,128)(2,1)S(1)}, u32[]{:S(2)}, u32[]{:S(2)}) collective-permute-start(bf16[12,2048]{1,0:T(8,128)(2,1)S(1)} %slice.6), channel_id=1, source_target_pairs={{0,64},{8,72},{16,80},{24,88},{32,96},{40,104},{48,112},{56,120},{... | collective-permute-start | bytes 147464
  300.6 21.7 %collective-permute-start.4 = (bf16[16,2048]{1,0:T(8,128)(2,1)S(1)}, bf16[16,2048]{1,0:T(8,128)(2,1)S(1)}, u32[]{:S(2)}, u32[]{:S(2)}) collective-permute-start(bf16[16,2048]{1,0:T(8,128)(2,1)S(1)} %fusion), channel_id=1, source_target_pairs={{0,40},{8,48},{16,56},{24,64},{32,72},{40,80},{48,88},{56,96},{64,... | collective-permute-start | bytes 196616
  302.5 19.7 %collective-permute-start.3 = (bf16[16,2048]{1,0:T(8,128)(2,1)S(1)}, bf16[16,2048]{1,0:T(8,128)(2,1)S(1)}, u32[]{:S(2)}, u32[]{:S(2)}) collective-permute-start(bf16[16,2048]{1,0:T(8,128)(2,1)S(1)} %fusion), channel_id=1, source_target_pairs={{0,32},{8,40},{16,48},{24,56},{32,64},{40,72},{48,80},{56,88},{64,... | collective-permute-start | bytes 196616
  311.7 10.6 %collective-permute-start.2 = (bf16[16,2048]{1,0:T(8,128)(2,1)S(1)}, bf16[16,2048]{1,0:T(8,128)(2,1)S(1)}, u32[]{:S(2)}, u32[]{:S(2)}) collective-permute-start(bf16[16,2048]{1,0:T(8,128)(2,1)S(1)} %fusion), channel_id=1, source_target_pairs={{0,24},{8,32},{16,40},{24,48},{32,56},{40,64},{48,72},{56,80},{64,... | collective-permute-start | bytes 196616
  313.6 10.9 %collective-permute-start.1 = (bf16[16,2048]{1,0:T(8,128)(2,1)S(1)}, bf16[16,2048]{1,0:T(8,128)(2,1)S(1)}, u32[]{:S(2)}, u32[]{:S(2)}) collective-permute-start(bf16[16,2048]{1,0:T(8,128)(2,1)S(1)} %fusion), channel_id=1, source_target_pairs={{0,16},{8,24},{16,32},{24,40},{32,48},{40,56},{48,64},{56,72},{64,... | collective-permute-start | bytes 196616
  317.6 8.3 %collective-permute-start = (bf16[16,2048]{1,0:T(8,128)(2,1)S(1)}, bf16[16,2048]{1,0:T(8,128)(2,1)S(1)}, u32[]{:S(2)}, u32[]{:S(2)}) collective-permute-start(bf16[16,2048]{1,0:T(8,128)(2,1)S(1)} %fusion), channel_id=1, source_target_pairs={{0,8},{8,16},{16,24},{24,32},{32,40},{40,48},{48,56},{56,64},{64,7... | collective-permute-start | bytes 196616
Sparse Core Ops, SparseCore 0:
  9.9 59.3 all-gather.1
  146.8 216.0 reduce-scatter.12
  366.8 214.3 reduce-scatter.10
  584.1 39.4 reduce-scatter.6
  626.6 39.2 reduce-scatter.8
